TPU v7x, 512 devices: a whole 4x4x16 slice. The times are simulated.
512 devices in a mesh: layer: 32 (over z, core), row: 16 (over y, x).
Axes of the slice: x: 4, y: 4, z: 16, core: 2. Of those that a mesh axis runs over, the one named last changes fastest.
Arguments:
- propagator: float32 [32, 16384, 6, 128], P('layer', 'row'), may hold values from -0.15625 to 0.15625
- col_blocks: int32 [32, 128, 6], P('layer', 'row'), may hold values from 0 to 127, as said below
- sources: bfloat16 [8, 32, 56, 16384], P(None, 'layer', None, 'row'), may hold values from -6 to 6
- incoming: bfloat16 [32, 56, 16384], P('layer', None, 'row'), may hold values from -6 to 6
Outputs:
- outgoing: bfloat16 [8, 32, 56, 16384], P(None, 'layer', None, 'row')
Inputs may be any that keep to these rules, and one draw needn't show every extreme that they name: col_blocks[l, r, k] differs from r by at most 8; slot 0 is r itself, slots 1 and 2 are r - 8 and r + 8 kept within 0 .. 127; entries of one row block may repeat.
All inputs are finite; a program needn't handle non-finite values.
Results may differ from a plain program's by a relative error of at most 0.0043.
Values may be sent and summed in bfloat16 or wider, within the bound.
A program may use at most 64 MiB of HBM per device.

v0:
```python
import jax
import jax.numpy as jnp
from jax import lax
from jax.sharding import PartitionSpec as P

BLK = 128
NBLK = 6
TICKS = 8


def with_halo(cells, sides, width):
    for axis, dim in sides:
        count = lax.axis_size(axis)
        ends = count - 1
        head = lax.slice_in_dim(cells, 0, width, axis=dim)
        tail = lax.slice_in_dim(cells, cells.shape[dim] - width, cells.shape[dim], axis=dim)
        cells = jnp.concatenate(
            [
                lax.ppermute(tail, axis, [(i, (i + 1) % count) for i in range(ends)]),
                cells,
                lax.ppermute(head, axis, [((i + 1) % count, i) for i in range(ends)]),
            ],
            axis=dim,
        )
    return cells


def from_behind(value, axis, by):
    size = lax.axis_size(axis)
    pairs = [(i, i + by) for i in range(size) if 0 <= i + by < size]
    return lax.ppermute(value, axis, pairs)


def apply_layer(layer_prop, local_cols, window, layer_source):
    shot_count, full_width = window.shape
    row_count = layer_prop.shape[0]
    blocks = window.reshape(shot_count, full_width // BLK, BLK)
    picked = blocks[:, local_cols, :].astype(jnp.float32)
    weights = layer_prop.reshape(row_count // BLK, BLK, NBLK, BLK)
    mixed_rows = jnp.einsum("srkc,rbkc->srb", picked, weights, precision=lax.Precision.HIGHEST)
    total = mixed_rows.reshape(shot_count, row_count) + layer_source.astype(jnp.float32)
    return total.astype(jnp.bfloat16)


def body(propagator, col_blocks, sources, incoming):
    layer_prop = propagator[0]
    layer_cols = col_blocks[0]
    row_count = layer_prop.shape[0]
    block_count = row_count // BLK
    row_place = lax.axis_index("row")
    near_cols = layer_cols - (row_place * block_count - block_count)
    current = incoming[0]
    window = current
    produced_all = []
    for tick_index in range(TICKS):
        window = with_halo(current, (("row", 1),), row_count)
        produced = apply_layer(layer_prop, near_cols, window, sources[tick_index, 0])
        produced_all.append(produced)
        if tick_index + 1 < TICKS:
            current = from_behind(produced, "layer", 1)
    return jnp.stack(produced_all)[:, None]


def solution(mesh):
    return jax.shard_map(
        body,
        mesh=mesh,
        in_specs=(
            P("layer", "row", None, None),
            P("layer", "row", None),
            P(None, "layer", None, "row"),
            P("layer", None, "row"),
        ),
        out_specs=P(None, "layer", None, "row"),
        check_vma=False,
    )
```

profile of v0, /device:TPU:249, one launch (start us, length us, event | category | flops | bytes accessed | tf_op | source)
XLA Modules:
  0.0 200.7 jit_solution(17128017681219005920)
XLA Ops:
  0.0 4.8 %collective-permute-start.1 = (bf16[56,1024]{1,0:T(8,128)(2,1)}, bf16[56,1024]{1,0:T(8,128)(2,1)S(1)}, u32[]{:S(2)}, u32[]{:S(2)}) collective-permute-start(bf16[56,1024]{1,0:T(8,128)(2,1)} %bitcast.282), channel_id=1, source_target_pairs={{1,0},{2,1},{3,2},{4,3},{5,4},{6,5},{7,6},{8,7},{9,8},{10,9},{11,1... | collective-permute-start | bytes 344072 | tf_op jit(solution)/shard_map/ppermute | solution.py:21
  4.8 1.9 collective-permute-start
  9.2 3.4 %collective-permute-done = bf16[56,1024]{1,0:T(8,128)(2,1)S(1)} collective-permute-done((bf16[56,1024]{1,0:T(8,128)(2,1)}, bf16[56,1024]{1,0:T(8,128)(2,1)S(1)}, u32[]{:S(2)}, u32[]{:S(2)}) %collective-permute-start) | collective-permute-done | bytes 114720 | tf_op jit(solution)/shard_map/ppermute | solution.py:19
  13.7 1.5 gather_fusion
  15.2 3.0 %fusion.14 = f32[8,56,128,1]{2,1,3,0:T(8,128)S(1)} fusion(bf16[56,8,6,128]{3,0,2,1:T(8,128)(2,1)} %bitcast.267, f32[8,128,6,128]{3,1,0,2:T(8,128)S(1)} %bitcast.258), kind=kOutput, calls=%fused_computation.22 | convolution fusion | flops 528482304 | bytes 4063232 | tf_op jit(solution)/shard_map/srkc,rbkc->srb/dot_general | solution.py:40
  19.2 6.7 %collective-permute-start.2 = (bf16[56,1024]{1,0:T(8,128)(2,1)S(1)}, bf16[56,1024]{1,0:T(8,128)(2,1)S(1)}, u32[]{:S(2)}, u32[]{:S(2)}) collective-permute-start(bf16[56,1024]{1,0:T(8,128)(2,1)S(1)} %fusion.22), channel_id=1, source_target_pairs={{0,16},{16,32},{32,48},{48,64},{64,80},{80,96},{96,112},{112,128},... | collective-permute-start | bytes 344072 | tf_op jit(solution)/shard_map/ppermute | solution.py:31
  26.0 1.8 collective-permute-done.2
  27.7 1.9 collective-permute-start.4
  29.7 3.4 %collective-permute-start.3 = (bf16[56,1024]{1,0:T(8,128)(2,1)S(1)}, bf16[56,1024]{1,0:T(8,128)(2,1)S(1)}, u32[]{:S(2)}, u32[]{:S(2)}) collective-permute-start(bf16[56,1024]{1,0:T(8,128)(2,1)S(1)} %collective-permute-done.2), channel_id=1, source_target_pairs={{0,1},{1,2},{2,3},{3,4},{4,5},{5,6},{6,7},{7,8},{8,9},{9,10},{10,1... | collective-permute-start | bytes 344072 | tf_op jit(solution)/shard_map/ppermute | solution.py:19
  33.0 1.6 collective-permute-done.4
  34.6 4.0 %collective-permute-done.3 = bf16[56,1024]{1,0:T(8,128)(2,1)S(1)} collective-permute-done((bf16[56,1024]{1,0:T(8,128)(2,1)S(1)}, bf16[56,1024]{1,0:T(8,128)(2,1)S(1)}, u32[]{:S(2)}, u32[]{:S(2)}) %collective-permute-start.3) | collective-permute-done | bytes 114720 | tf_op jit(solution)/shard_map/ppermute | solution.py:19
  38.7 1.5 gather_fusion.1
  40.3 3.0 %fusion.12 = f32[8,56,128,1]{2,1,3,0:T(8,128)S(1)} fusion(bf16[56,8,6,128]{3,0,2,1:T(8,128)(2,1)} %bitcast.268, f32[8,128,6,128]{3,1,0,2:T(8,128)S(1)} %bitcast.265), kind=kOutput, calls=%fused_computation.20 | convolution fusion | flops 528482304 | bytes 4063232 | tf_op jit(solution)/shard_map/srkc,rbkc->srb/dot_general | solution.py:40
  44.3 5.3 %collective-permute-start.5 = (bf16[56,1024]{1,0:T(8,128)(2,1)S(1)}, bf16[56,1024]{1,0:T(8,128)(2,1)S(1)}, u32[]{:S(2)}, u32[]{:S(2)}) collective-permute-start(bf16[56,1024]{1,0:T(8,128)(2,1)S(1)} %fusion.26), channel_id=1, source_target_pairs={{0,16},{16,32},{32,48},{48,64},{64,80},{80,96},{96,112},{112,128},... | collective-permute-start | bytes 344072 | tf_op jit(solution)/shard_map/ppermute | solution.py:31
  49.6 1.8 collective-permute-done.5
  51.4 1.9 collective-permute-start.7
  53.3 3.4 %collective-permute-start.6 = (bf16[56,1024]{1,0:T(8,128)(2,1)S(1)}, bf16[56,1024]{1,0:T(8,128)(2,1)S(1)}, u32[]{:S(2)}, u32[]{:S(2)}) collective-permute-start(bf16[56,1024]{1,0:T(8,128)(2,1)S(1)} %collective-permute-done.5), channel_id=1, source_target_pairs={{0,1},{1,2},{2,3},{3,4},{4,5},{5,6},{6,7},{7,8},{8,9},{9,10},{10,1... | collective-permute-start | bytes 344072 | tf_op jit(solution)/shard_map/ppermute | solution.py:19
  56.7 1.7 collective-permute-done.7
  58.4 4.0 %collective-permute-done.6 = bf16[56,1024]{1,0:T(8,128)(2,1)S(1)} collective-permute-done((bf16[56,1024]{1,0:T(8,128)(2,1)S(1)}, bf16[56,1024]{1,0:T(8,128)(2,1)S(1)}, u32[]{:S(2)}, u32[]{:S(2)}) %collective-permute-start.6) | collective-permute-done | bytes 114720 | tf_op jit(solution)/shard_map/ppermute | solution.py:19
  62.5 1.5 gather_fusion.2
  64.1 3.0 %fusion.10 = f32[8,56,128,1]{2,1,3,0:T(8,128)S(1)} fusion(bf16[56,8,6,128]{3,0,2,1:T(8,128)(2,1)} %bitcast.269, f32[8,128,6,128]{3,1,0,2:T(8,128)S(1)} %bitcast.264), kind=kOutput, calls=%fused_computation.18 | convolution fusion | flops 528482304 | bytes 4063232 | tf_op jit(solution)/shard_map/srkc,rbkc->srb/dot_general | solution.py:40
  68.1 5.2 %collective-permute-start.8 = (bf16[56,1024]{1,0:T(8,128)(2,1)S(1)}, bf16[56,1024]{1,0:T(8,128)(2,1)S(1)}, u32[]{:S(2)}, u32[]{:S(2)}) collective-permute-start(bf16[56,1024]{1,0:T(8,128)(2,1)S(1)} %fusion.30), channel_id=1, source_target_pairs={{0,16},{16,32},{32,48},{48,64},{64,80},{80,96},{96,112},{112,128},... | collective-permute-start | bytes 344072 | tf_op jit(solution)/shard_map/ppermute | solution.py:31
  73.3 1.8 collective-permute-done.8
  75.1 1.9 collective-permute-start.10
  77.0 3.4 %collective-permute-start.9 = (bf16[56,1024]{1,0:T(8,128)(2,1)S(1)}, bf16[56,1024]{1,0:T(8,128)(2,1)S(1)}, u32[]{:S(2)}, u32[]{:S(2)}) collective-permute-start(bf16[56,1024]{1,0:T(8,128)(2,1)S(1)} %collective-permute-done.8), channel_id=1, source_target_pairs={{0,1},{1,2},{2,3},{3,4},{4,5},{5,6},{6,7},{7,8},{8,9},{9,10},{10,1... | collective-permute-start | bytes 344072 | tf_op jit(solution)/shard_map/ppermute | solution.py:19
  80.4 1.7 collective-permute-done.10
  82.1 4.0 %collective-permute-done.9 = bf16[56,1024]{1,0:T(8,128)(2,1)S(1)} collective-permute-done((bf16[56,1024]{1,0:T(8,128)(2,1)S(1)}, bf16[56,1024]{1,0:T(8,128)(2,1)S(1)}, u32[]{:S(2)}, u32[]{:S(2)}) %collective-permute-start.9) | collective-permute-done | bytes 114720 | tf_op jit(solution)/shard_map/ppermute | solution.py:19
  87.7 3.1 %fusion.8 = f32[8,56,128,1]{2,1,3,0:T(8,128)S(1)} fusion(bf16[56,8,6,128]{3,0,2,1:T(8,128)(2,1)} %bitcast.270, f32[8,128,6,128]{3,1,0,2:T(8,128)S(1)} %bitcast.263), kind=kOutput, calls=%fused_computation.16 | convolution fusion | flops 528482304 | bytes 4063232 | tf_op jit(solution)/shard_map/srkc,rbkc->srb/dot_general | solution.py:40
  92.4 5.2 %collective-permute-start.11 = (bf16[56,1024]{1,0:T(8,128)(2,1)S(1)}, bf16[56,1024]{1,0:T(8,128)(2,1)}, u32[]{:S(2)}, u32[]{:S(2)}) collective-permute-start(bf16[56,1024]{1,0:T(8,128)(2,1)S(1)} %fusion.34), channel_id=1, source_target_pairs={{0,16},{16,32},{32,48},{48,64},{64,80},{80,96},{96,112},{112,128},... | collective-permute-start | bytes 344072 | tf_op jit(solution)/shard_map/ppermute | solution.py:31
  98.4 1.7 reshape.299
  100.0 1.9 collective-permute-start.13
  101.9 3.4 %collective-permute-start.12 = (bf16[56,1024]{1,0:T(8,128)(2,1)}, bf16[56,1024]{1,0:T(8,128)(2,1)}, u32[]{:S(2)}, u32[]{:S(2)}) collective-permute-start(bf16[56,1024]{1,0:T(8,128)(2,1)} %collective-permute-done.11), channel_id=1, source_target_pairs={{0,1},{1,2},{2,3},{3,4},{4,5},{5,6},{6,7},{7,8},{8,9},{9,10},{10,1... | collective-permute-start | bytes 344072 | tf_op jit(solution)/shard_map/ppermute | solution.py:19
  105.3 1.7 fusion.55
  107.7 1.7 reshape.302
  111.7 1.5 gather_fusion.4
  113.3 3.1 %fusion.6 = f32[8,56,128,1]{2,1,3,0:T(8,128)S(1)} fusion(bf16[56,8,6,128]{3,0,2,1:T(8,128)(2,1)} %bitcast.271, f32[8,128,6,128]{3,1,0,2:T(8,128)S(1)} %bitcast.262), kind=kOutput, calls=%fused_computation.14 | convolution fusion | flops 528482304 | bytes 4063232 | tf_op jit(solution)/shard_map/srkc,rbkc->srb/dot_general | solution.py:40
  117.9 5.4 %collective-permute-start.14 = (bf16[56,1024]{1,0:T(8,128)(2,1)S(1)}, bf16[56,1024]{1,0:T(8,128)(2,1)}, u32[]{:S(2)}, u32[]{:S(2)}) collective-permute-start(bf16[56,1024]{1,0:T(8,128)(2,1)S(1)} %fusion.38), channel_id=1, source_target_pairs={{0,16},{16,32},{32,48},{48,64},{64,80},{80,96},{96,112},{112,128},... | collective-permute-start | bytes 344072 | tf_op jit(solution)/shard_map/ppermute | solution.py:31
  123.4 1.6 fusion.54
  125.7 1.7 reshape.305
  127.4 3.3 %collective-permute-start.16 = (bf16[56,1024]{1,0:T(8,128)(2,1)}, bf16[56,1024]{1,0:T(8,128)(2,1)S(1)}, u32[]{:S(2)}, u32[]{:S(2)}) collective-permute-start(bf16[56,1024]{1,0:T(8,128)(2,1)} %collective-permute-done.14), channel_id=1, source_target_pairs={{1,0},{2,1},{3,2},{4,3},{5,4},{6,5},{7,6},{8,7},{9,8},{10,9},{11,1... | collective-permute-start | bytes 344072 | tf_op jit(solution)/shard_map/ppermute | solution.py:21
  130.7 2.2 %collective-permute-start.15 = (bf16[56,1024]{1,0:T(8,128)(2,1)}, bf16[56,1024]{1,0:T(8,128)(2,1)}, u32[]{:S(2)}, u32[]{:S(2)}) collective-permute-start(bf16[56,1024]{1,0:T(8,128)(2,1)} %collective-permute-done.14), channel_id=1, source_target_pairs={{0,1},{1,2},{2,3},{3,4},{4,5},{5,6},{6,7},{7,8},{8,9},{9,10},{10,1... | collective-permute-start | bytes 344072 | tf_op jit(solution)/shard_map/ppermute | solution.py:19
  132.9 1.7 fusion.53
  135.3 1.7 reshape.308
  139.7 1.5 gather_fusion.5
  141.3 3.1 %fusion.4 = f32[8,56,128,1]{2,1,3,0:T(8,128)S(1)} fusion(bf16[56,8,6,128]{3,0,2,1:T(8,128)(2,1)} %bitcast.272, f32[8,128,6,128]{3,1,0,2:T(8,128)S(1)} %bitcast.261), kind=kOutput, calls=%fused_computation.12 | convolution fusion | flops 528482304 | bytes 4063232 | tf_op jit(solution)/shard_map/srkc,rbkc->srb/dot_general | solution.py:40
  145.3 4.9 %collective-permute-start.17 = (bf16[56,1024]{1,0:T(8,128)(2,1)S(1)}, bf16[56,1024]{1,0:T(8,128)(2,1)}, u32[]{:S(2)}, u32[]{:S(2)}) collective-permute-start(bf16[56,1024]{1,0:T(8,128)(2,1)S(1)} %fusion.42), channel_id=1, source_target_pairs={{0,16},{16,32},{32,48},{48,64},{64,80},{80,96},{96,112},{112,128},... | collective-permute-start | bytes 344072 | tf_op jit(solution)/shard_map/ppermute | solution.py:31
  150.2 1.6 fusion.52
  152.5 1.7 reshape.311
  154.1 3.5 %collective-permute-start.19 = (bf16[56,1024]{1,0:T(8,128)(2,1)}, bf16[56,1024]{1,0:T(8,128)(2,1)S(1)}, u32[]{:S(2)}, u32[]{:S(2)}) collective-permute-start(bf16[56,1024]{1,0:T(8,128)(2,1)} %collective-permute-done.17), channel_id=1, source_target_pairs={{1,0},{2,1},{3,2},{4,3},{5,4},{6,5},{7,6},{8,7},{9,8},{10,9},{11,1... | collective-permute-start | bytes 344072 | tf_op jit(solution)/shard_map/ppermute | solution.py:21
  157.6 1.9 collective-permute-start.18
  159.5 1.7 fusion.51
  161.9 1.7 reshape.314
  164.3 1.7 collective-permute-done.18
  167.0 1.5 gather_fusion.6
  168.6 3.0 %fusion.2 = f32[8,56,128,1]{2,1,3,0:T(8,128)S(1)} fusion(bf16[56,8,6,128]{3,0,2,1:T(8,128)(2,1)} %bitcast.273, f32[8,128,6,128]{3,1,0,2:T(8,128)S(1)} %bitcast.260), kind=kOutput, calls=%fused_computation.10 | convolution fusion | flops 528482304 | bytes 4063232 | tf_op jit(solution)/shard_map/srkc,rbkc->srb/dot_general | solution.py:40
  172.6 4.5 %collective-permute-start.20 = (bf16[56,1024]{1,0:T(8,128)(2,1)S(1)}, bf16[56,1024]{1,0:T(8,128)(2,1)}, u32[]{:S(2)}, u32[]{:S(2)}) collective-permute-start(bf16[56,1024]{1,0:T(8,128)(2,1)S(1)} %fusion.46), channel_id=1, source_target_pairs={{0,16},{16,32},{32,48},{48,64},{64,80},{80,96},{96,112},{112,128},... | collective-permute-start | bytes 344072 | tf_op jit(solution)/shard_map/ppermute | solution.py:31
  177.1 1.6 fusion.50
  180.4 3.3 %collective-permute-start.22 = (bf16[56,1024]{1,0:T(8,128)(2,1)}, bf16[56,1024]{1,0:T(8,128)(2,1)S(1)}, u32[]{:S(2)}, u32[]{:S(2)}) collective-permute-start(bf16[56,1024]{1,0:T(8,128)(2,1)} %collective-permute-done.20), channel_id=1, source_target_pairs={{1,0},{2,1},{3,2},{4,3},{5,4},{6,5},{7,6},{8,7},{9,8},{10,9},{11,1... | collective-permute-start | bytes 344072 | tf_op jit(solution)/shard_map/ppermute | solution.py:21
  183.7 2.0 collective-permute-start.21
  185.7 1.6 fusion.49
  187.2 4.7 %collective-permute-done.21 = bf16[56,1024]{1,0:T(8,128)(2,1)S(1)} collective-permute-done((bf16[56,1024]{1,0:T(8,128)(2,1)}, bf16[56,1024]{1,0:T(8,128)(2,1)S(1)}, u32[]{:S(2)}, u32[]{:S(2)}) %collective-permute-start.21) | collective-permute-done | bytes 114720 | tf_op jit(solution)/shard_map/ppermute | solution.py:19
  192.9 1.5 gather_fusion.7
  194.4 3.0 %fusion.16 = f32[56,8,128]{2,0,1:T(8,128)S(1)} fusion(bf16[56,8,6,128]{3,0,2,1:T(8,128)(2,1)} %bitcast.266, f32[8,128,6,128]{3,1,0,2:T(8,128)S(1)} %bitcast.259), kind=kOutput, calls=%fused_computation.24 | convolution fusion | flops 528482304 | bytes 4063232 | tf_op jit(solution)/shard_map/srkc,rbkc->srb/dot_general | solution.py:40
  199.1 1.6 fusion.48
  (79 shorter events, 28.8 us)
Async XLA Ops:
  0.0 15.2 %copy-start = (f32[1,1024,6,128]{3,1,2,0:T(8,128)S(1)}, f32[1,1024,6,128]{3,1,2,0:T(8,128)}, u32[]{:S(2)}) copy-start(f32[1,1024,6,128]{3,1,2,0:T(8,128)} %param.4) | copy-start | bytes 9437188
  0.0 9.2 %collective-permute-start.1 = (bf16[56,1024]{1,0:T(8,128)(2,1)}, bf16[56,1024]{1,0:T(8,128)(2,1)S(1)}, u32[]{:S(2)}, u32[]{:S(2)}) collective-permute-start(bf16[56,1024]{1,0:T(8,128)(2,1)} %bitcast.282), channel_id=1, source_target_pairs={{1,0},{2,1},{3,2},{4,3},{5,4},{6,5},{7,6},{8,7},{9,8},{10,9},{11,1... | collective-permute-start | bytes 344072 | tf_op jit(solution)/shard_map/ppermute | solution.py:21
  4.8 7.9 %collective-permute-start = (bf16[56,1024]{1,0:T(8,128)(2,1)}, bf16[56,1024]{1,0:T(8,128)(2,1)S(1)}, u32[]{:S(2)}, u32[]{:S(2)}) collective-permute-start(bf16[56,1024]{1,0:T(8,128)(2,1)} %bitcast.283), channel_id=1, source_target_pairs={{0,1},{1,2},{2,3},{3,4},{4,5},{5,6},{6,7},{7,8},{8,9},{9,10},{10,1... | collective-permute-start | bytes 344072 | tf_op jit(solution)/shard_map/ppermute | solution.py:19
  18.2 16.4 %copy-start.1 = (f32[8,56,128,1]{2,1,3,0:T(8,128)}, f32[8,56,128,1]{2,1,3,0:T(8,128)S(1)}, u32[]{:S(2)}) copy-start(f32[8,56,128,1]{2,1,3,0:T(8,128)S(1)} %fusion.14) | copy-start | bytes 688132
  19.2 8.5 %collective-permute-start.2 = (bf16[56,1024]{1,0:T(8,128)(2,1)S(1)}, bf16[56,1024]{1,0:T(8,128)(2,1)S(1)}, u32[]{:S(2)}, u32[]{:S(2)}) collective-permute-start(bf16[56,1024]{1,0:T(8,128)(2,1)S(1)} %fusion.22), channel_id=1, source_target_pairs={{0,16},{16,32},{32,48},{48,64},{64,80},{80,96},{96,112},{112,128},... | collective-permute-start | bytes 344072 | tf_op jit(solution)/shard_map/ppermute | solution.py:31
  27.7 6.9 %collective-permute-start.4 = (bf16[56,1024]{1,0:T(8,128)(2,1)S(1)}, bf16[56,1024]{1,0:T(8,128)(2,1)S(1)}, u32[]{:S(2)}, u32[]{:S(2)}) collective-permute-start(bf16[56,1024]{1,0:T(8,128)(2,1)S(1)} %collective-permute-done.2), channel_id=1, source_target_pairs={{1,0},{2,1},{3,2},{4,3},{5,4},{6,5},{7,6},{8,7},{9,8},{10,9},{11,1... | collective-permute-start | bytes 344072 | tf_op jit(solution)/shard_map/ppermute | solution.py:21
  29.7 9.0 %collective-permute-start.3 = (bf16[56,1024]{1,0:T(8,128)(2,1)S(1)}, bf16[56,1024]{1,0:T(8,128)(2,1)S(1)}, u32[]{:S(2)}, u32[]{:S(2)}) collective-permute-start(bf16[56,1024]{1,0:T(8,128)(2,1)S(1)} %collective-permute-done.2), channel_id=1, source_target_pairs={{0,1},{1,2},{2,3},{3,4},{4,5},{5,6},{6,7},{7,8},{8,9},{9,10},{10,1... | collective-permute-start | bytes 344072 | tf_op jit(solution)/shard_map/ppermute | solution.py:19
  43.3 15.2 %copy-start.3 = (f32[8,56,128,1]{2,1,3,0:T(8,128)}, f32[8,56,128,1]{2,1,3,0:T(8,128)S(1)}, u32[]{:S(2)}) copy-start(f32[8,56,128,1]{2,1,3,0:T(8,128)S(1)} %fusion.12) | copy-start | bytes 688132
  44.3 7.1 %collective-permute-start.5 = (bf16[56,1024]{1,0:T(8,128)(2,1)S(1)}, bf16[56,1024]{1,0:T(8,128)(2,1)S(1)}, u32[]{:S(2)}, u32[]{:S(2)}) collective-permute-start(bf16[56,1024]{1,0:T(8,128)(2,1)S(1)} %fusion.26), channel_id=1, source_target_pairs={{0,16},{16,32},{32,48},{48,64},{64,80},{80,96},{96,112},{112,128},... | collective-permute-start | bytes 344072 | tf_op jit(solution)/shard_map/ppermute | solution.py:31
  51.4 7.0 %collective-permute-start.7 = (bf16[56,1024]{1,0:T(8,128)(2,1)S(1)}, bf16[56,1024]{1,0:T(8,128)(2,1)S(1)}, u32[]{:S(2)}, u32[]{:S(2)}) collective-permute-start(bf16[56,1024]{1,0:T(8,128)(2,1)S(1)} %collective-permute-done.5), channel_id=1, source_target_pairs={{1,0},{2,1},{3,2},{4,3},{5,4},{6,5},{7,6},{8,7},{9,8},{10,9},{11,1... | collective-permute-start | bytes 344072 | tf_op jit(solution)/shard_map/ppermute | solution.py:21
  53.3 9.2 %collective-permute-start.6 = (bf16[56,1024]{1,0:T(8,128)(2,1)S(1)}, bf16[56,1024]{1,0:T(8,128)(2,1)S(1)}, u32[]{:S(2)}, u32[]{:S(2)}) collective-permute-start(bf16[56,1024]{1,0:T(8,128)(2,1)S(1)} %collective-permute-done.5), channel_id=1, source_target_pairs={{0,1},{1,2},{2,3},{3,4},{4,5},{5,6},{6,7},{7,8},{8,9},{9,10},{10,1... | collective-permute-start | bytes 344072 | tf_op jit(solution)/shard_map/ppermute | solution.py:19
  67.1 15.0 %copy-start.5 = (f32[8,56,128,1]{2,1,3,0:T(8,128)}, f32[8,56,128,1]{2,1,3,0:T(8,128)S(1)}, u32[]{:S(2)}) copy-start(f32[8,56,128,1]{2,1,3,0:T(8,128)S(1)} %fusion.10) | copy-start | bytes 688132
  68.1 7.0 %collective-permute-start.8 = (bf16[56,1024]{1,0:T(8,128)(2,1)S(1)}, bf16[56,1024]{1,0:T(8,128)(2,1)S(1)}, u32[]{:S(2)}, u32[]{:S(2)}) collective-permute-start(bf16[56,1024]{1,0:T(8,128)(2,1)S(1)} %fusion.30), channel_id=1, source_target_pairs={{0,16},{16,32},{32,48},{48,64},{64,80},{80,96},{96,112},{112,128},... | collective-permute-start | bytes 344072 | tf_op jit(solution)/shard_map/ppermute | solution.py:31
  75.1 7.0 %collective-permute-start.10 = (bf16[56,1024]{1,0:T(8,128)(2,1)S(1)}, bf16[56,1024]{1,0:T(8,128)(2,1)S(1)}, u32[]{:S(2)}, u32[]{:S(2)}) collective-permute-start(bf16[56,1024]{1,0:T(8,128)(2,1)S(1)} %collective-permute-done.8), channel_id=1, source_target_pairs={{1,0},{2,1},{3,2},{4,3},{5,4},{6,5},{7,6},{8,7},{9,8},{10,9},{11,1... | collective-permute-start | bytes 344072 | tf_op jit(solution)/shard_map/ppermute | solution.py:21
  77.0 9.1 %collective-permute-start.9 = (bf16[56,1024]{1,0:T(8,128)(2,1)S(1)}, bf16[56,1024]{1,0:T(8,128)(2,1)S(1)}, u32[]{:S(2)}, u32[]{:S(2)}) collective-permute-start(bf16[56,1024]{1,0:T(8,128)(2,1)S(1)} %collective-permute-done.8), channel_id=1, source_target_pairs={{0,1},{1,2},{2,3},{3,4},{4,5},{5,6},{6,7},{7,8},{8,9},{9,10},{10,1... | collective-permute-start | bytes 344072 | tf_op jit(solution)/shard_map/ppermute | solution.py:19
  87.7 9.9 %copy-start.2 = (f32[8,56,128,1]{2,1,3,0:T(8,128)S(1)}, f32[8,56,128,1]{2,1,3,0:T(8,128)}, u32[]{:S(2)}) copy-start(f32[8,56,128,1]{2,1,3,0:T(8,128)} %copy-done.1) | copy-start | bytes 688132
  87.7 19.3 %copy-start.4 = (f32[8,56,128,1]{2,1,3,0:T(8,128)S(1)}, f32[8,56,128,1]{2,1,3,0:T(8,128)}, u32[]{:S(2)}) copy-start(f32[8,56,128,1]{2,1,3,0:T(8,128)} %copy-done.3) | copy-start | bytes 688132
  90.8 0.7 copy-start.7
  92.4 7.6 %collective-permute-start.11 = (bf16[56,1024]{1,0:T(8,128)(2,1)S(1)}, bf16[56,1024]{1,0:T(8,128)(2,1)}, u32[]{:S(2)}, u32[]{:S(2)}) collective-permute-start(bf16[56,1024]{1,0:T(8,128)(2,1)S(1)} %fusion.34), channel_id=1, source_target_pairs={{0,16},{16,32},{32,48},{48,64},{64,80},{80,96},{96,112},{112,128},... | collective-permute-start | bytes 344072 | tf_op jit(solution)/shard_map/ppermute | solution.py:31
  100.0 9.4 %collective-permute-start.13 = (bf16[56,1024]{1,0:T(8,128)(2,1)}, bf16[56,1024]{1,0:T(8,128)(2,1)S(1)}, u32[]{:S(2)}, u32[]{:S(2)}) collective-permute-start(bf16[56,1024]{1,0:T(8,128)(2,1)} %collective-permute-done.11), channel_id=1, source_target_pairs={{1,0},{2,1},{3,2},{4,3},{5,4},{6,5},{7,6},{8,7},{9,8},{10,9},{11,1... | collective-permute-start | bytes 344072 | tf_op jit(solution)/shard_map/ppermute | solution.py:21
  101.9 8.7 %collective-permute-start.12 = (bf16[56,1024]{1,0:T(8,128)(2,1)}, bf16[56,1024]{1,0:T(8,128)(2,1)}, u32[]{:S(2)}, u32[]{:S(2)}) collective-permute-start(bf16[56,1024]{1,0:T(8,128)(2,1)} %collective-permute-done.11), channel_id=1, source_target_pairs={{0,1},{1,2},{2,3},{3,4},{4,5},{5,6},{6,7},{7,8},{8,9},{9,10},{10,1... | collective-permute-start | bytes 344072 | tf_op jit(solution)/shard_map/ppermute | solution.py:19
  109.4 0.6 copy-start.16
  113.2 10.2 %copy-start.11 = (f32[1,56,1024]{2,1,0:T(8,128)S(1)}, f32[1,56,1024]{2,1,0:T(8,128)}, u32[]{:S(2)}) copy-start(f32[1,56,1024]{2,1,0:T(8,128)} %reshape.302) | copy-start | bytes 688132
  113.2 11.7 %copy-start.6 = (f32[8,56,128,1]{2,1,3,0:T(8,128)S(1)}, f32[8,56,128,1]{2,1,3,0:T(8,128)}, u32[]{:S(2)}) copy-start(f32[8,56,128,1]{2,1,3,0:T(8,128)} %copy-done.5) | copy-start | bytes 688132
  113.3 21.3 %copy-start.8 = (f32[8,56,128,1]{2,1,3,0:T(8,128)S(1)}, f32[8,56,128,1]{2,1,3,0:T(8,128)}, u32[]{:S(2)}) copy-start(f32[8,56,128,1]{2,1,3,0:T(8,128)} %copy-done.7) | copy-start | bytes 688132
  116.3 0.7 copy-start.9
  117.9 9.4 %collective-permute-start.14 = (bf16[56,1024]{1,0:T(8,128)(2,1)S(1)}, bf16[56,1024]{1,0:T(8,128)(2,1)}, u32[]{:S(2)}, u32[]{:S(2)}) collective-permute-start(bf16[56,1024]{1,0:T(8,128)(2,1)S(1)} %fusion.38), channel_id=1, source_target_pairs={{0,16},{16,32},{32,48},{48,64},{64,80},{80,96},{96,112},{112,128},... | collective-permute-start | bytes 344072 | tf_op jit(solution)/shard_map/ppermute | solution.py:31
  127.4 9.6 %collective-permute-start.16 = (bf16[56,1024]{1,0:T(8,128)(2,1)}, bf16[56,1024]{1,0:T(8,128)(2,1)S(1)}, u32[]{:S(2)}, u32[]{:S(2)}) collective-permute-start(bf16[56,1024]{1,0:T(8,128)(2,1)} %collective-permute-done.14), channel_id=1, source_target_pairs={{1,0},{2,1},{3,2},{4,3},{5,4},{6,5},{7,6},{8,7},{9,8},{10,9},{11,1... | collective-permute-start | bytes 344072 | tf_op jit(solution)/shard_map/ppermute | solution.py:21
  130.7 8.0 %collective-permute-start.15 = (bf16[56,1024]{1,0:T(8,128)(2,1)}, bf16[56,1024]{1,0:T(8,128)(2,1)}, u32[]{:S(2)}, u32[]{:S(2)}) collective-permute-start(bf16[56,1024]{1,0:T(8,128)(2,1)} %collective-permute-done.14), channel_id=1, source_target_pairs={{0,1},{1,2},{2,3},{3,4},{4,5},{5,6},{6,7},{7,8},{8,9},{9,10},{10,1... | collective-permute-start | bytes 344072 | tf_op jit(solution)/shard_map/ppermute | solution.py:19
  136.9 0.6 copy-start.14
  141.3 8.9 %copy-start.12 = (f32[1,56,1024]{2,1,0:T(8,128)S(1)}, f32[1,56,1024]{2,1,0:T(8,128)}, u32[]{:S(2)}) copy-start(f32[1,56,1024]{2,1,0:T(8,128)} %reshape.308) | copy-start | bytes 688132
  141.3 10.5 %copy-start.10 = (f32[8,56,128,1]{2,1,3,0:T(8,128)S(1)}, f32[8,56,128,1]{2,1,3,0:T(8,128)}, u32[]{:S(2)}) copy-start(f32[8,56,128,1]{2,1,3,0:T(8,128)} %copy-done.9) | copy-start | bytes 688132
  145.3 8.9 %collective-permute-start.17 = (bf16[56,1024]{1,0:T(8,128)(2,1)S(1)}, bf16[56,1024]{1,0:T(8,128)(2,1)}, u32[]{:S(2)}, u32[]{:S(2)}) collective-permute-start(bf16[56,1024]{1,0:T(8,128)(2,1)S(1)} %fusion.42), channel_id=1, source_target_pairs={{0,16},{16,32},{32,48},{48,64},{64,80},{80,96},{96,112},{112,128},... | collective-permute-start | bytes 344072 | tf_op jit(solution)/shard_map/ppermute | solution.py:31
  154.1 9.5 %collective-permute-start.19 = (bf16[56,1024]{1,0:T(8,128)(2,1)}, bf16[56,1024]{1,0:T(8,128)(2,1)S(1)}, u32[]{:S(2)}, u32[]{:S(2)}) collective-permute-start(bf16[56,1024]{1,0:T(8,128)(2,1)} %collective-permute-done.17), channel_id=1, source_target_pairs={{1,0},{2,1},{3,2},{4,3},{5,4},{6,5},{7,6},{8,7},{9,8},{10,9},{11,1... | collective-permute-start | bytes 344072 | tf_op jit(solution)/shard_map/ppermute | solution.py:21
  157.6 8.3 %collective-permute-start.18 = (bf16[56,1024]{1,0:T(8,128)(2,1)}, bf16[56,1024]{1,0:T(8,128)(2,1)}, u32[]{:S(2)}, u32[]{:S(2)}) collective-permute-start(bf16[56,1024]{1,0:T(8,128)(2,1)} %collective-permute-done.17), channel_id=1, source_target_pairs={{0,1},{1,2},{2,3},{3,4},{4,5},{5,6},{6,7},{7,8},{8,9},{9,10},{10,1... | collective-permute-start | bytes 344072 | tf_op jit(solution)/shard_map/ppermute | solution.py:19
  163.6 0.6 copy-start.15
  168.6 8.5 %copy-start.13 = (f32[1,56,1024]{2,1,0:T(8,128)S(1)}, f32[1,56,1024]{2,1,0:T(8,128)}, u32[]{:S(2)}) copy-start(f32[1,56,1024]{2,1,0:T(8,128)} %reshape.314) | copy-start | bytes 688132
  172.6 7.8 %collective-permute-start.20 = (bf16[56,1024]{1,0:T(8,128)(2,1)S(1)}, bf16[56,1024]{1,0:T(8,128)(2,1)}, u32[]{:S(2)}, u32[]{:S(2)}) collective-permute-start(bf16[56,1024]{1,0:T(8,128)(2,1)S(1)} %fusion.46), channel_id=1, source_target_pairs={{0,16},{16,32},{32,48},{48,64},{64,80},{80,96},{96,112},{112,128},... | collective-permute-start | bytes 344072 | tf_op jit(solution)/shard_map/ppermute | solution.py:31
  180.4 6.9 %collective-permute-start.22 = (bf16[56,1024]{1,0:T(8,128)(2,1)}, bf16[56,1024]{1,0:T(8,128)(2,1)S(1)}, u32[]{:S(2)}, u32[]{:S(2)}) collective-permute-start(bf16[56,1024]{1,0:T(8,128)(2,1)} %collective-permute-done.20), channel_id=1, source_target_pairs={{1,0},{2,1},{3,2},{4,3},{5,4},{6,5},{7,6},{8,7},{9,8},{10,9},{11,1... | collective-permute-start | bytes 344072 | tf_op jit(solution)/shard_map/ppermute | solution.py:21
  183.7 8.2 %collective-permute-start.21 = (bf16[56,1024]{1,0:T(8,128)(2,1)}, bf16[56,1024]{1,0:T(8,128)(2,1)S(1)}, u32[]{:S(2)}, u32[]{:S(2)}) collective-permute-start(bf16[56,1024]{1,0:T(8,128)(2,1)} %collective-permute-done.20), channel_id=1, source_target_pairs={{0,1},{1,2},{2,3},{3,4},{4,5},{5,6},{6,7},{7,8},{8,9},{9,10},{10,1... | collective-permute-start | bytes 344072 | tf_op jit(solution)/shard_map/ppermute | solution.py:19
where the time goes:
time: 202 us; the launch traced here: 201 us
  starting transfers between devices  81.2 us (40%)
  local copies, waits for them, and re-layouts  35.2 us (17%)
  waiting for transfers between devices  34 us (17%)
  other arithmetic  25.6 us (13%)
  matrix products  24.3 us (12%)
    ppermute x7, starting transfers between devices, from_behind(): return lax.ppermute(value, axis, pairs)  37.3 us
    dot_general x8, matrix products, apply_layer(): jnp.einsum('srkc,rbkc->srb', picked, weights, precision=lax.Precision.HIG...  24.3 us
    ppermute x8, waiting for transfers between devices, with_halo(): lax.ppermute(tail, axis, [(i, (i + 1) % count) for i in range(ends)])  23.5 us
    ppermute x8, starting transfers between devices, with_halo(): lax.ppermute(head, axis, [((i + 1) % count, i) for i in range(ends)])  22.5 us
    ppermute x8, starting transfers between devices, with_halo(): lax.ppermute(tail, axis, [(i, (i + 1) % count) for i in range(ends)])  21.4 us
    gather x8, local copies, waits for them, and re-layouts, apply_layer(): picked = blocks[:, local_cols, :].astype(jnp.float32)  12.3 us
    reshape x8, local copies, waits for them, and re-layouts, apply_layer(): mixed_rows.reshape(shot_count, row_count) + layer_source.astype(jnp.float32)  12 us
    unnamed x7, other arithmetic  11.3 us
  transfers between devices with their start and end apart: 23, of which 14 were waited for; matrix products, arithmetic and copies ran while one was open for 15% of the time, Pallas kernels for 0%

commit v1 on v0

v1 whole, which is shorter than its diff:
```python
import jax
import jax.numpy as jnp
from jax import lax
from jax.experimental import pallas as pl
from jax.experimental.pallas import tpu as pltpu
from jax.sharding import PartitionSpec as P

BLK = 128
NBLK = 6
TICKS = 8
SLOTS = 4
CHUNKS = ((0, 16), (16, 16), (32, 16), (48, 8))
MESH = pl.DeviceIdType.MESH


def kernel(
    prop_hbm, cols_hbm, src_hbm, inc_hbm, out_hbm,
    prop, weights, cols, src, win, cur, obuf,
    prop_sem, cols_sem, src_sem, inc_sem, out_sem, send_sem, recv_sem, halo_send, halo_recv,
):
    layers = lax.axis_size("layer")
    places = lax.axis_size("row")
    layer = lax.axis_index("layer")
    place = lax.axis_index("row")
    width = obuf.shape[2]
    row_blocks = width // BLK
    has_left = place > 0
    has_right = place < places - 1
    has_next = layer < layers - 1
    has_prev = layer > 0

    inc_copy = pltpu.make_async_copy(inc_hbm.at[0], win.at[0, place % SLOTS], inc_sem)
    inc_copy.start()
    cols_copy = pltpu.make_async_copy(cols_hbm, cols, cols_sem)
    cols_copy.start()
    prop_copies = []
    for j in range(row_blocks):
        rows = pl.ds(j * BLK, BLK)
        prop_copies.append(
            pltpu.make_async_copy(prop_hbm.at[:, rows, :], prop.at[:, rows, :], prop_sem.at[j])
        )
        prop_copies[-1].start()
    src_copy = pltpu.make_async_copy(src_hbm.at[:, 0], src, src_sem)
    src_copy.start()

    barrier = pltpu.get_barrier_semaphore()

    def greet(ok, to_layer, to_place):
        @pl.when(ok)
        def _():
            pl.semaphore_signal(
                barrier, inc=1, device_id={"layer": to_layer, "row": to_place}, device_id_type=MESH
            )

    greet(has_left, layer, place - 1)
    greet(has_right, layer, place + 1)
    greet(has_prev, layer - 1, place)
    greet(jnp.logical_and(has_prev, has_left), layer - 1, place - 1)
    greet(jnp.logical_and(has_prev, has_right), layer - 1, place + 1)
    left_n = has_left.astype(jnp.int32)
    right_n = has_right.astype(jnp.int32)
    next_n = has_next.astype(jnp.int32)
    pl.semaphore_wait(barrier, left_n + right_n + next_n * (1 + left_n + right_n))

    inc_copy.wait()

    sides = ((has_left, -1), (has_right, 1))
    slot = place % SLOTS

    def halo(c, side):
        start, size = CHUNKS[c]
        ok, step = sides[side]
        rows = pl.ds(start, size)
        return ok, pltpu.make_async_remote_copy(
            src_ref=win.at[0, slot, rows, :],
            dst_ref=win.at[0, slot, rows, :],
            send_sem=halo_send.at[c, side],
            recv_sem=halo_recv.at[c, side],
            device_id={"layer": layer, "row": place + step},
            device_id_type=MESH,
        )

    for c in range(len(CHUNKS)):
        for side in range(2):
            ok, copy = halo(c, side)
            pl.when(ok)(copy.start)

    for j in range(row_blocks):
        prop_copies[j].wait()
        for k in range(NBLK):
            value = prop[k, j * BLK : (j + 1) * BLK, :]
            high = value.astype(jnp.bfloat16)
            low = (value - high.astype(jnp.float32)).astype(jnp.bfloat16)
            weights[j, 0:BLK, k * BLK : (k + 1) * BLK] = high
            weights[j, BLK : 2 * BLK, k * BLK : (k + 1) * BLK] = low

    @pl.when(layer == 0)
    def _():
        win[1:] = jnp.zeros((TICKS - 1,) + win.shape[1:], win.dtype)

    cols_copy.wait()
    picks = [[lax.rem(cols[k, 0, j], SLOTS * row_blocks) for k in range(NBLK)] for j in range(row_blocks)]
    src_copy.wait()

    targets = (
        (has_next, 0),
        (jnp.logical_and(has_next, has_left), -1),
        (jnp.logical_and(has_next, has_right), 1),
    )

    def forward(tick, c, which):
        start, size = CHUNKS[c]
        ok, step = targets[which]
        rows = pl.ds(start, size)
        return ok, pltpu.make_async_remote_copy(
            src_ref=obuf.at[tick, rows, :],
            dst_ref=win.at[(tick + 1) % TICKS, slot, rows, :],
            send_sem=send_sem.at[tick, c, which],
            recv_sem=recv_sem.at[tick, c, which],
            device_id={"layer": layer + 1, "row": place + step},
            device_id_type=MESH,
        )

    def store_out(tick, c):
        start, size = CHUNKS[c]
        rows = pl.ds(start, size)
        return pltpu.make_async_copy(obuf.at[tick, rows, :], out_hbm.at[tick, 0, rows, :], out_sem.at[tick, c])

    def compute(tick, c):
        start, size = CHUNKS[c]
        for step in (-1, 0, 1):
            near = (place + step + SLOTS) % SLOTS
            for b in range(row_blocks):
                cur[near * row_blocks + b, 0:size, :] = win[tick, near, start : start + size, b * BLK : (b + 1) * BLK]
        for j in range(row_blocks):
            picked = jnp.concatenate([cur[picks[j][k], 0:size, :] for k in range(NBLK)], axis=1)
            mixed = lax.dot_general(
                picked, weights[j], (((1,), (1,)), ((), ())), preferred_element_type=jnp.float32
            )
            total = mixed[:, 0:BLK] + mixed[:, BLK : 2 * BLK]
            added = src[tick, start : start + size, j * BLK : (j + 1) * BLK].astype(jnp.float32)
            obuf[tick, start : start + size, j * BLK : (j + 1) * BLK] = (total + added).astype(jnp.bfloat16)
        store_out(tick, c).start()

    for c in range(len(CHUNKS)):
        for side in range(2):
            ok = (has_right, has_left)[side]
            pl.when(ok)(halo(c, side)[1].wait_recv)
        compute(0, c)
        for which in range(3):
            ok, copy = forward(0, c, which)
            pl.when(ok)(copy.start)

    arrives = (
        has_prev,
        jnp.logical_and(has_prev, has_right),
        jnp.logical_and(has_prev, has_left),
    )

    @pl.loop(1, TICKS)
    def _(tick):
        for c in range(len(CHUNKS)):
            for which in range(3):
                pl.when(arrives[which])(forward(tick - 1, c, which)[1].wait_recv)
            compute(tick, c)
            for which in range(3):
                ok, copy = forward(tick, c, which)
                pl.when(jnp.logical_and(ok, tick < TICKS - 1))(copy.start)

    for c in range(len(CHUNKS)):
        for side in range(2):
            ok, copy = halo(c, side)
            pl.when(ok)(copy.wait_send)

    @pl.loop(0, TICKS)
    def _(tick):
        for c in range(len(CHUNKS)):
            for which in range(3):
                ok, copy = forward(tick, c, which)
                pl.when(jnp.logical_and(ok, tick < TICKS - 1))(copy.wait_send)
            store_out(tick, c).wait()


def body(propagator, col_blocks, sources, incoming):
    rows = propagator.shape[1]
    shots = incoming.shape[1]
    prop = jnp.transpose(propagator[0], (1, 0, 2))
    cols = jnp.transpose(col_blocks, (2, 0, 1))
    chunks = len(CHUNKS)
    return pl.pallas_call(
        kernel,
        name="sweep",
        out_shape=jax.ShapeDtypeStruct(sources.shape, jnp.bfloat16),
        in_specs=[pl.BlockSpec(memory_space=pl.ANY)] * 4,
        out_specs=pl.BlockSpec(memory_space=pl.ANY),
        scratch_shapes=[
            pltpu.VMEM((NBLK, rows, BLK), jnp.float32),
            pltpu.VMEM((rows // BLK, 2 * BLK, NBLK * BLK), jnp.bfloat16),
            pltpu.SMEM(cols.shape, jnp.int32),
            pltpu.VMEM((TICKS, shots, rows), jnp.bfloat16),
            pltpu.VMEM((TICKS, SLOTS, shots, rows), jnp.bfloat16),
            pltpu.VMEM((SLOTS * rows // BLK, 16, BLK), jnp.bfloat16),
            pltpu.VMEM((TICKS, shots, rows), jnp.bfloat16),
            pltpu.SemaphoreType.DMA((rows // BLK,)),
            pltpu.SemaphoreType.DMA,
            pltpu.SemaphoreType.DMA,
            pltpu.SemaphoreType.DMA,
            pltpu.SemaphoreType.DMA((TICKS, chunks)),
            pltpu.SemaphoreType.DMA((TICKS, chunks, 3)),
            pltpu.SemaphoreType.DMA((TICKS, chunks, 3)),
            pltpu.SemaphoreType.DMA((chunks, 2)),
            pltpu.SemaphoreType.DMA((chunks, 2)),
        ],
        compiler_params=pltpu.CompilerParams(collective_id=0, has_side_effects=True),
    )(prop, cols, sources, incoming)


def solution(mesh):
    return jax.shard_map(
        body,
        mesh=mesh,
        in_specs=(
            P("layer", "row", None, None),
            P("layer", "row", None),
            P(None, "layer", None, "row"),
            P("layer", None, "row"),
        ),
        out_specs=P(None, "layer", None, "row"),
        check_vma=False,
    )
```

time: 202 us -> 55.2 us (0.27)
  the two profiles are of different devices: /device:TPU:249 before, /device:TPU:504 now
where the time goes in v1:
time: 55.2 us; the launch traced here: 55 us
  Pallas kernels  52.9 us (96%)
  local copies, waits for them, and re-layouts  2.16 us (4%)
    pallas_call x1, Pallas kernels, body(): pl.pallas_call(kernel, name='sweep', out_shape=jax.ShapeDtypeStruct(sourc...  52.9 us
    unnamed x1, local copies, waits for them, and re-layouts  2.16 us

profile of v1, /device:TPU:504, one launch (start us, length us, event | category | flops | bytes accessed | tf_op | source)
XLA Modules:
  0.0 55.0 jit_solution(11299584519195816451)
XLA Ops:
  0.0 52.9 %sweep.1 = bf16[8,1,56,1024]{3,2,1,0:T(8,128)(2,1)} custom-call(f32[6,1024,128]{2,1,0:T(8,128)} %bitcast.4, s32[6,1,8]{2,1,0:T(1,128)} %bitcast.5, bf16[8,1,56,1024]{3,2,1,0:T(8,128)(2,1)} %src_hbm.1, bf16[1,56,1024]{2,1,0:T(8,128)(2,1)} %inc_hbm.1), custom_call_target="tpu_custom_call" | custom-call | tf_op jit(solution)/shard_map/sweep/pallas_call | solution.py:190
  52.9 2.2 %copy.6 = bf16[8,1,56,1024]{3,2,1,0:T(8,128)(2,1)} copy(bf16[8,1,56,1024]{3,2,1,0:T(8,128)(2,1)} %sweep.1) | data formatting | bytes 1835008

commit v2 on v1

v2 whole, which is shorter than its diff:
```python
import jax
import jax.numpy as jnp
from jax import lax
from jax.experimental import pallas as pl
from jax.experimental.pallas import tpu as pltpu
from jax.sharding import PartitionSpec as P

BLK = 128
NBLK = 6
TICKS = 8
SLOTS = 4
GROUP = 8
MESH = pl.DeviceIdType.MESH


def kernel(
    prop_hbm, cols_hbm, src_hbm, inc_hbm, out_hbm,
    prop, weights, cols, src, win, cur, obuf,
    prop_sem, cols_sem, src_sem, inc_sem, out_sem, send_sem, recv_sem, halo_send,
):
    layers = lax.axis_size("layer")
    places = lax.axis_size("row")
    layer = lax.axis_index("layer")
    place = lax.axis_index("row")
    steps, group, width = obuf.shape
    chunks = steps // TICKS
    row_blocks = width // BLK
    slot = place % SLOTS
    has_left = place > 0
    has_right = place < places - 1
    has_next = layer < layers - 1
    has_prev = layer > 0

    inc_copy = pltpu.make_async_copy(inc_hbm, win.at[pl.ds(0, chunks), slot], inc_sem)
    inc_copy.start()
    cols_copy = pltpu.make_async_copy(cols_hbm, cols, cols_sem)
    cols_copy.start()
    prop_copies = []
    for j in range(row_blocks):
        rows = pl.ds(j * BLK, BLK)
        prop_copies.append(
            pltpu.make_async_copy(prop_hbm.at[:, rows, :], prop.at[:, rows, :], prop_sem.at[j])
        )
        prop_copies[-1].start()
    src_copy = pltpu.make_async_copy(src_hbm, src, src_sem)
    src_copy.start()

    barrier = pltpu.get_barrier_semaphore()

    def greet(ok, to_layer, to_place):
        @pl.when(ok)
        def _():
            pl.semaphore_signal(
                barrier, inc=1, device_id={"layer": to_layer, "row": to_place}, device_id_type=MESH
            )

    greet(has_prev & has_left, layer - 1, place - 1)
    greet(has_prev & has_right, layer - 1, place + 1)
    greet(has_left, layer, place - 1)
    greet(has_right, layer, place + 1)
    greet(has_prev, layer - 1, place)

    for j in range(row_blocks):
        prop_copies[j].wait()
        for k in range(NBLK):
            value = prop[k, j * BLK : (j + 1) * BLK, :].T
            high = value.astype(jnp.bfloat16)
            low = (value - high.astype(jnp.float32)).astype(jnp.bfloat16)
            weights[j, k * BLK : (k + 1) * BLK, 0:BLK] = high
            weights[j, k * BLK : (k + 1) * BLK, BLK : 2 * BLK] = low

    left_n = has_left.astype(jnp.int32)
    right_n = has_right.astype(jnp.int32)
    next_n = has_next.astype(jnp.int32)
    pl.semaphore_wait(barrier, left_n + right_n + next_n * (1 + left_n + right_n))

    inc_copy.wait()

    def halo(c, side):
        return pltpu.make_async_remote_copy(
            src_ref=win.at[c, slot],
            dst_ref=win.at[c, slot],
            send_sem=halo_send.at[c, side],
            recv_sem=recv_sem.at[c, side],
            device_id={"layer": layer, "row": place + (-1, 1)[side]},
            device_id_type=MESH,
        )

    for c in range(chunks):
        pl.when(has_left)(halo(c, 0).start)
        pl.when(has_right)(halo(c, 1).start)

    @pl.when(layer == 0)
    def _():
        win[chunks:] = jnp.zeros((steps - chunks,) + win.shape[1:], win.dtype)

    cols_copy.wait()
    picks = [[lax.rem(cols[k, 0, j], SLOTS * row_blocks) for k in range(NBLK)] for j in range(row_blocks)]
    src_copy.wait()

    def forward(step, which):
        return pltpu.make_async_remote_copy(
            src_ref=obuf.at[step],
            dst_ref=win.at[(step + chunks) % steps, slot],
            send_sem=send_sem.at[step, which],
            recv_sem=recv_sem.at[(step + chunks) % steps, which],
            device_id={"layer": layer + 1, "row": place + (-1, 1, 0)[which]},
            device_id_type=MESH,
        )

    def arrival(step, which):
        return pltpu.make_async_remote_copy(
            src_ref=win.at[step, slot],
            dst_ref=win.at[step, slot],
            send_sem=send_sem.at[step, which],
            recv_sem=recv_sem.at[step, which],
            device_id={"layer": layer, "row": place},
            device_id_type=MESH,
        )

    def store_out(step):
        return pltpu.make_async_copy(obuf.at[step], out_hbm.at[step], out_sem.at[step])

    sends = ((0, has_next & has_left), (1, has_next & has_right), (2, has_next))

    @pl.loop(0, steps)
    def _(step):
        first = step < chunks
        pl.when((first | has_prev) & has_right)(arrival(step, 0).wait_recv)
        pl.when((first | has_prev) & has_left)(arrival(step, 1).wait_recv)
        pl.when(jnp.logical_not(first) & has_prev)(arrival(step, 2).wait_recv)
        for shift in (-1, 0, 1):
            near = (place + shift + SLOTS) % SLOTS
            for b in range(row_blocks):
                cur[near * row_blocks + b] = win[step, near, :, b * BLK : (b + 1) * BLK]
        for j in range(row_blocks):
            picked = jnp.concatenate([cur[picks[j][k]] for k in range(NBLK)], axis=1)
            mixed = lax.dot_general(
                picked, weights[j], (((1,), (0,)), ((), ())), preferred_element_type=jnp.float32
            )
            total = mixed[:, 0:BLK] + mixed[:, BLK : 2 * BLK]
            added = src[step, :, j * BLK : (j + 1) * BLK].astype(jnp.float32)
            obuf[step, :, j * BLK : (j + 1) * BLK] = (total + added).astype(jnp.bfloat16)
        more = step < steps - chunks
        for which, ok in sends:
            pl.when(ok & more)(forward(step, which).start)
        store_out(step).start()

    for c in range(chunks):
        pl.when(has_left)(halo(c, 0).wait_send)
        pl.when(has_right)(halo(c, 1).wait_send)

    @pl.loop(0, steps)
    def _(step):
        more = step < steps - chunks
        for which, ok in sends:
            pl.when(ok & more)(forward(step, which).wait_send)
        store_out(step).wait()


def body(propagator, col_blocks, sources, incoming):
    rows = propagator.shape[1]
    ticks, _, shots, _ = sources.shape
    chunks = shots // GROUP
    steps = ticks * chunks
    prop = jnp.transpose(propagator[0], (1, 0, 2))
    cols = jnp.transpose(col_blocks, (2, 0, 1))
    out = pl.pallas_call(
        kernel,
        name="sweep",
        out_shape=jax.ShapeDtypeStruct((steps, GROUP, rows), jnp.bfloat16),
        in_specs=[pl.BlockSpec(memory_space=pl.ANY)] * 4,
        out_specs=pl.BlockSpec(memory_space=pl.ANY),
        scratch_shapes=[
            pltpu.VMEM((NBLK, rows, BLK), jnp.float32),
            pltpu.VMEM((rows // BLK, NBLK * BLK, 2 * BLK), jnp.bfloat16),
            pltpu.SMEM(cols.shape, jnp.int32),
            pltpu.VMEM((steps, GROUP, rows), jnp.bfloat16),
            pltpu.VMEM((steps, SLOTS, GROUP, rows), jnp.bfloat16),
            pltpu.VMEM((SLOTS * rows // BLK, GROUP, BLK), jnp.bfloat16),
            pltpu.VMEM((steps, GROUP, rows), jnp.bfloat16),
            pltpu.SemaphoreType.DMA((rows // BLK,)),
            pltpu.SemaphoreType.DMA,
            pltpu.SemaphoreType.DMA,
            pltpu.SemaphoreType.DMA,
            pltpu.SemaphoreType.DMA((steps,)),
            pltpu.SemaphoreType.DMA((steps, 3)),
            pltpu.SemaphoreType.DMA((steps, 3)),
            pltpu.SemaphoreType.DMA((chunks, 2)),
        ],
        compiler_params=pltpu.CompilerParams(collective_id=0, has_side_effects=True),
    )(
        prop,
        cols,
        sources.reshape(steps, GROUP, rows),
        incoming.reshape(chunks, GROUP, rows),
    )
    return out.reshape(sources.shape)


def solution(mesh):
    return jax.shard_map(
        body,
        mesh=mesh,
        in_specs=(
            P("layer", "row", None, None),
            P("layer", "row", None),
            P(None, "layer", None, "row"),
            P("layer", None, "row"),
        ),
        out_specs=P(None, "layer", None, "row"),
        check_vma=False,
    )
```

time: 55.2 us -> 49.7 us (0.900)
  the two profiles are of different devices: /device:TPU:504 before, /device:TPU:441 now
where the time goes in v2:
time: 49.7 us; the launch traced here: 49.6 us
  Pallas kernels  47.4 us (95%)
  local copies, waits for them, and re-layouts  2.16 us (4%)
    pallas_call x1, Pallas kernels, body(): pl.pallas_call(kernel, name='sweep', out_shape=jax.ShapeDtypeStruct((step...  47.4 us
    unnamed x1, local copies, waits for them, and re-layouts  2.16 us

profile of v2, /device:TPU:441, one launch (start us, length us, event | category | flops | bytes accessed | tf_op | source)
XLA Modules:
  0.0 49.6 jit_solution(13593839799536743338)
XLA Ops:
  0.0 47.4 %sweep.1 = bf16[56,8,1024]{2,1,0:T(8,128)(2,1)} custom-call(f32[6,1024,128]{2,1,0:T(8,128)} %bitcast.10, s32[6,1,8]{2,1,0:T(1,128)} %bitcast.13, bf16[56,8,1024]{2,1,0:T(8,128)(2,1)} %bitcast.11, bf16[7,8,1024]{2,1,0:T(8,128)(2,1)} %bitcast.12), custom_call_target="tpu_custom_call" | custom-call | tf_op jit(solution)/shard_map/sweep/pallas_call | solution.py:168
  47.4 2.2 %copy.7 = bf16[8,1,56,1024]{3,2,1,0:T(8,128)(2,1)} copy(bf16[8,1,56,1024]{3,2,1,0:T(8,128)(2,1)} %bitcast.9) | data formatting | bytes 1835008

commit v3 on v2

--- a/solution.py
+++ b/solution.py
@@ -14,9 +14,9 @@
 
 
 def kernel(
-    prop_hbm, cols_hbm, src_hbm, inc_hbm, out_hbm,
-    prop, weights, cols, src, win, cur, obuf,
-    prop_sem, cols_sem, src_sem, inc_sem, out_sem, send_sem, recv_sem, halo_send,
+    prop_hbm, cols_hbm, src_hbm, inc_hbm, obuf,
+    prop, weights, cols, src, win, cur,
+    prop_sem, cols_sem, src_sem, inc_sem, send_sem, recv_sem, halo_send,
 ):
     layers = lax.axis_size("layer")
     places = lax.axis_size("row")
@@ -28,6 +28,7 @@
     slot = place % SLOTS
     has_left = place > 0
     has_right = place < places - 1
+    inner = has_left & has_right
     has_next = layer < layers - 1
     has_prev = layer > 0
 
@@ -60,15 +61,17 @@
     greet(has_right, layer, place + 1)
     greet(has_prev, layer - 1, place)
 
-    for j in range(row_blocks):
-        prop_copies[j].wait()
-        for k in range(NBLK):
-            value = prop[k, j * BLK : (j + 1) * BLK, :].T
-            high = value.astype(jnp.bfloat16)
-            low = (value - high.astype(jnp.float32)).astype(jnp.bfloat16)
-            weights[j, k * BLK : (k + 1) * BLK, 0:BLK] = high
-            weights[j, k * BLK : (k + 1) * BLK, BLK : 2 * BLK] = low
-
+    def prepare(blocks):
+        for j in blocks:
+            prop_copies[j].wait()
+            for k in range(NBLK):
+                value = prop[k, j * BLK : (j + 1) * BLK, :].T
+                high = value.astype(jnp.bfloat16)
+                low = (value - high.astype(jnp.float32)).astype(jnp.bfloat16)
+                weights[j, k * BLK : (k + 1) * BLK, 0:BLK] = high
+                weights[j, k * BLK : (k + 1) * BLK, BLK : 2 * BLK] = low
+
+    prepare(range(0, row_blocks // 2))
     left_n = has_left.astype(jnp.int32)
     right_n = has_right.astype(jnp.int32)
     next_n = has_next.astype(jnp.int32)
@@ -80,8 +83,8 @@
         return pltpu.make_async_remote_copy(
             src_ref=win.at[c, slot],
             dst_ref=win.at[c, slot],
-            send_sem=halo_send.at[c, side],
-            recv_sem=recv_sem.at[c, side],
+            send_sem=halo_send.at[side],
+            recv_sem=recv_sem.at[c],
             device_id={"layer": layer, "row": place + (-1, 1)[side]},
             device_id_type=MESH,
         )
@@ -89,6 +92,8 @@
     for c in range(chunks):
         pl.when(has_left)(halo(c, 0).start)
         pl.when(has_right)(halo(c, 1).start)
+
+    prepare(range(row_blocks // 2, row_blocks))
 
     @pl.when(layer == 0)
     def _():
@@ -102,33 +107,25 @@
         return pltpu.make_async_remote_copy(
             src_ref=obuf.at[step],
             dst_ref=win.at[(step + chunks) % steps, slot],
-            send_sem=send_sem.at[step, which],
-            recv_sem=recv_sem.at[(step + chunks) % steps, which],
+            send_sem=send_sem.at[which],
+            recv_sem=recv_sem.at[(step + chunks) % steps],
             device_id={"layer": layer + 1, "row": place + (-1, 1, 0)[which]},
             device_id_type=MESH,
         )
 
-    def arrival(step, which):
-        return pltpu.make_async_remote_copy(
-            src_ref=win.at[step, slot],
-            dst_ref=win.at[step, slot],
-            send_sem=send_sem.at[step, which],
-            recv_sem=recv_sem.at[step, which],
-            device_id={"layer": layer, "row": place},
-            device_id_type=MESH,
-        )
-
-    def store_out(step):
-        return pltpu.make_async_copy(obuf.at[step], out_hbm.at[step], out_sem.at[step])
+    def take(step, pieces):
+        pieces = win.at[step, pl.ds(0, pieces)]
+        pltpu.make_async_copy(pieces, pieces, recv_sem.at[step]).wait()
 
     sends = ((0, has_next & has_left), (1, has_next & has_right), (2, has_next))
 
     @pl.loop(0, steps)
     def _(step):
         first = step < chunks
-        pl.when((first | has_prev) & has_right)(arrival(step, 0).wait_recv)
-        pl.when((first | has_prev) & has_left)(arrival(step, 1).wait_recv)
-        pl.when(jnp.logical_not(first) & has_prev)(arrival(step, 2).wait_recv)
+        later = jnp.logical_not(first) & has_prev
+        pl.when(later & inner)(lambda: take(step, 3))
+        pl.when((later & jnp.logical_not(inner)) | (first & inner))(lambda: take(step, 2))
+        pl.when(first & jnp.logical_not(inner))(lambda: take(step, 1))
         for shift in (-1, 0, 1):
             near = (place + shift + SLOTS) % SLOTS
             for b in range(row_blocks):
@@ -144,18 +141,18 @@
         more = step < steps - chunks
         for which, ok in sends:
             pl.when(ok & more)(forward(step, which).start)
-        store_out(step).start()
-
-    for c in range(chunks):
-        pl.when(has_left)(halo(c, 0).wait_send)
-        pl.when(has_right)(halo(c, 1).wait_send)
-
-    @pl.loop(0, steps)
-    def _(step):
-        more = step < steps - chunks
-        for which, ok in sends:
-            pl.when(ok & more)(forward(step, which).wait_send)
-        store_out(step).wait()
+
+    def drained(ref, sem):
+        pltpu.make_async_copy(ref, ref, sem).wait()
+
+    for side, ok in ((0, has_left), (1, has_right)):
+        pl.when(ok)(lambda: drained(win.at[pl.ds(0, chunks), slot], halo_send.at[side]))
+    for which, ok in sends:
+        pl.when(ok)(lambda: drained(obuf.at[pl.ds(0, steps - chunks)], send_sem.at[which]))
+
+
+def stay(x):
+    return pltpu.with_memory_space_constraint(x, pltpu.MemorySpace.HBM)
 
 
 def body(propagator, col_blocks, sources, incoming):
@@ -170,7 +167,7 @@
         name="sweep",
         out_shape=jax.ShapeDtypeStruct((steps, GROUP, rows), jnp.bfloat16),
         in_specs=[pl.BlockSpec(memory_space=pl.ANY)] * 4,
-        out_specs=pl.BlockSpec(memory_space=pl.ANY),
+        out_specs=pl.BlockSpec(memory_space=pltpu.VMEM),
         scratch_shapes=[
             pltpu.VMEM((NBLK, rows, BLK), jnp.float32),
             pltpu.VMEM((rows // BLK, NBLK * BLK, 2 * BLK), jnp.bfloat16),
@@ -178,22 +175,20 @@
             pltpu.VMEM((steps, GROUP, rows), jnp.bfloat16),
             pltpu.VMEM((steps, SLOTS, GROUP, rows), jnp.bfloat16),
             pltpu.VMEM((SLOTS * rows // BLK, GROUP, BLK), jnp.bfloat16),
-            pltpu.VMEM((steps, GROUP, rows), jnp.bfloat16),
             pltpu.SemaphoreType.DMA((rows // BLK,)),
             pltpu.SemaphoreType.DMA,
             pltpu.SemaphoreType.DMA,
             pltpu.SemaphoreType.DMA,
+            pltpu.SemaphoreType.DMA((3,)),
             pltpu.SemaphoreType.DMA((steps,)),
-            pltpu.SemaphoreType.DMA((steps, 3)),
-            pltpu.SemaphoreType.DMA((steps, 3)),
-            pltpu.SemaphoreType.DMA((chunks, 2)),
+            pltpu.SemaphoreType.DMA((2,)),
         ],
-        compiler_params=pltpu.CompilerParams(collective_id=0, has_side_effects=True),
+        compiler_params=pltpu.CompilerParams(collective_id=0, has_side_effects=True, vmem_limit_bytes=14 << 20),
     )(
-        prop,
-        cols,
-        sources.reshape(steps, GROUP, rows),
-        incoming.reshape(chunks, GROUP, rows),
+        stay(prop),
+        stay(cols),
+        stay(sources.reshape(steps, GROUP, rows)),
+        stay(incoming.reshape(chunks, GROUP, rows)),
     )
     return out.reshape(sources.shape)
 

time: 49.7 us -> 44.8 us (0.901)
  Pallas kernels: 47.4 us -> 43.6 us
  local copies, waits for them, and re-layouts: 2.16 us -> 0.93 us
    pallas_call x1, Pallas kernels: 47.4 us -> 43.6 us  [body(): pl.pallas_call(kernel, name='sweep', out_shape=jax.ShapeDtypeStruct((step...]
    unnamed x1, local copies, waits for them, and re-layouts: 2.16 us -> 0.93 us
where the time goes in v3:
time: 44.8 us; the launch traced here: 44.6 us
  Pallas kernels  43.6 us (97%)
  local copies, waits for them, and re-layouts  0.93 us (2%)
    pallas_call x1, Pallas kernels, body(): pl.pallas_call(kernel, name='sweep', out_shape=jax.ShapeDtypeStruct((step...  43.6 us
    unnamed x1, local copies, waits for them, and re-layouts  0.93 us

profile of v3, /device:TPU:441, one launch (start us, length us, event | category | flops | bytes accessed | tf_op | source)
XLA Modules:
  0.0 44.6 jit_solution(13425847048915960052)
XLA Ops:
  0.0 43.6 %sweep.1 = bf16[56,8,1024]{2,1,0:T(8,128)(2,1)S(1)} custom-call(f32[6,1024,128]{2,1,0:T(8,128)} %bitcast.10, s32[6,1,8]{2,1,0:T(1,128)} %bitcast.13, bf16[56,8,1024]{2,1,0:T(8,128)(2,1)} %bitcast.11, bf16[7,8,1024]{2,1,0:T(8,128)(2,1)} %bitcast.12), custom_call_target="tpu_custom_call" | custom-call | tf_op jit(solution)/shard_map/sweep/pallas_call | solution.py:165
  43.7 0.9 %copy.7 = bf16[8,1,56,1024]{3,2,1,0:T(8,128)(2,1)} copy(bf16[8,1,56,1024]{3,2,1,0:T(8,128)(2,1)S(1)} %bitcast.9) | data formatting | bytes 1835008

commit v4 on v3

--- a/solution.py
+++ b/solution.py
@@ -55,8 +55,6 @@
                 barrier, inc=1, device_id={"layer": to_layer, "row": to_place}, device_id_type=MESH
             )
 
-    greet(has_prev & has_left, layer - 1, place - 1)
-    greet(has_prev & has_right, layer - 1, place + 1)
     greet(has_left, layer, place - 1)
     greet(has_right, layer, place + 1)
     greet(has_prev, layer - 1, place)
@@ -66,16 +64,12 @@
             prop_copies[j].wait()
             for k in range(NBLK):
                 value = prop[k, j * BLK : (j + 1) * BLK, :].T
-                high = value.astype(jnp.bfloat16)
-                low = (value - high.astype(jnp.float32)).astype(jnp.bfloat16)
-                weights[j, k * BLK : (k + 1) * BLK, 0:BLK] = high
-                weights[j, k * BLK : (k + 1) * BLK, BLK : 2 * BLK] = low
-
-    prepare(range(0, row_blocks // 2))
+                weights[j, k * BLK : (k + 1) * BLK, :] = value.astype(jnp.bfloat16)
+
     left_n = has_left.astype(jnp.int32)
     right_n = has_right.astype(jnp.int32)
     next_n = has_next.astype(jnp.int32)
-    pl.semaphore_wait(barrier, left_n + right_n + next_n * (1 + left_n + right_n))
+    pl.semaphore_wait(barrier, left_n + right_n + next_n)
 
     inc_copy.wait()
 
@@ -93,7 +87,7 @@
         pl.when(has_left)(halo(c, 0).start)
         pl.when(has_right)(halo(c, 1).start)
 
-    prepare(range(row_blocks // 2, row_blocks))
+    prepare(range(row_blocks))
 
     @pl.when(layer == 0)
     def _():
@@ -135,7 +129,7 @@
             mixed = lax.dot_general(
                 picked, weights[j], (((1,), (0,)), ((), ())), preferred_element_type=jnp.float32
             )
-            total = mixed[:, 0:BLK] + mixed[:, BLK : 2 * BLK]
+            total = mixed
             added = src[step, :, j * BLK : (j + 1) * BLK].astype(jnp.float32)
             obuf[step, :, j * BLK : (j + 1) * BLK] = (total + added).astype(jnp.bfloat16)
         more = step < steps - chunks
@@ -170,7 +164,7 @@
         out_specs=pl.BlockSpec(memory_space=pltpu.VMEM),
         scratch_shapes=[
             pltpu.VMEM((NBLK, rows, BLK), jnp.float32),
-            pltpu.VMEM((rows // BLK, NBLK * BLK, 2 * BLK), jnp.bfloat16),
+            pltpu.VMEM((rows // BLK, NBLK * BLK, BLK), jnp.bfloat16),
             pltpu.SMEM(cols.shape, jnp.int32),
             pltpu.VMEM((steps, GROUP, rows), jnp.bfloat16),
             pltpu.VMEM((steps, SLOTS, GROUP, rows), jnp.bfloat16),

time: 44.8 us -> 42.7 us (0.953)
  Pallas kernels: 43.6 us -> 41.7 us
    pallas_call x1, Pallas kernels: 43.6 us -> 41.7 us  [body(): pl.pallas_call(kernel, name='sweep', out_shape=jax.ShapeDtypeStruct((step...]
where the time goes in v4:
time: 42.7 us; the launch traced here: 42.6 us
  Pallas kernels  41.7 us (98%)
  local copies, waits for them, and re-layouts  0.93 us (2%)
    pallas_call x1, Pallas kernels, body(): pl.pallas_call(kernel, name='sweep', out_shape=jax.ShapeDtypeStruct((step...  41.7 us
    unnamed x1, local copies, waits for them, and re-layouts  0.93 us

profile of v4, /device:TPU:441, one launch (start us, length us, event | category | flops | bytes accessed | tf_op | source)
XLA Modules:
  0.0 42.6 jit_solution(4231791841144812024)
XLA Ops:
  0.0 41.7 %sweep.1 = bf16[56,8,1024]{2,1,0:T(8,128)(2,1)S(1)} custom-call(f32[6,1024,128]{2,1,0:T(8,128)} %bitcast.10, s32[6,1,8]{2,1,0:T(1,128)} %bitcast.13, bf16[56,8,1024]{2,1,0:T(8,128)(2,1)} %bitcast.11, bf16[7,8,1024]{2,1,0:T(8,128)(2,1)} %bitcast.12), custom_call_target="tpu_custom_call" | custom-call | tf_op jit(solution)/shard_map/sweep/pallas_call | solution.py:159
  41.7 0.9 %copy.7 = bf16[8,1,56,1024]{3,2,1,0:T(8,128)(2,1)} copy(bf16[8,1,56,1024]{3,2,1,0:T(8,128)(2,1)S(1)} %bitcast.9) | data formatting | bytes 1835008
